TPU v7x, 32 devices: a whole 2x2x4 slice. The times are simulated.
32 devices in a mesh: st: 8 (over z, y), ob: 4 (over x, core).
Axes of the slice: x: 2, y: 2, z: 4, core: 2. Of those that a mesh axis runs over, the one named last changes fastest.
Arguments:
- ensemble: bfloat16 [18432, 64], P('st'), may hold values from -3 to 3
- weights: bfloat16 [4096, 64], P('ob'), may hold values from -6 to 6
- obs_column: int32 [4096], P('ob'), may hold values from 0 to 18431
Outputs:
- forecast: float32 [64, 3, 48, 128], P('ob', None, 'st')
All inputs are finite; a program needn't handle non-finite values.
Results may differ from a plain program's by a relative error of at most 0.0061.
Values may be sent and summed in bfloat16 or wider, within the bound.
A program may use at most 128 MiB of HBM per device.

v0:
```python
import jax
import jax.numpy as jnp
from jax import lax
from jax.sharding import PartitionSpec as P

NLON = 128
STEPS = 3
MEMBERS_PER_PART = 16
time_step = 0.3


def with_halo(block, sides, width):
    for axis, dim in sides:
        count = lax.axis_size(axis)
        forward = [(i, i + 1) for i in range(count - 1)]
        backward = [(target, source) for source, target in forward]
        low = lax.ppermute(
            lax.slice_in_dim(block, block.shape[dim] - width, None, axis=dim), axis, forward
        )
        high = lax.ppermute(lax.slice_in_dim(block, 0, width, axis=dim), axis, backward)
        block = jnp.concatenate([low, block, high], axis=dim)
    return block


def tapering(state_rows, columns, radius):
    state_lat = state_rows // (3 * NLON)
    state_lon = state_rows % NLON
    obs_lat = columns // (3 * NLON)
    obs_lon = columns % NLON
    lat_gap = state_lat[:, None] - obs_lat[None, :]
    lon_gap = jnp.abs(state_lon[:, None] - obs_lon[None, :])
    lon_gap = jnp.minimum(lon_gap, NLON - lon_gap)
    squared = (lat_gap * lat_gap + lon_gap * lon_gap).astype(jnp.float32)
    falloff = jnp.maximum(jnp.float32(0.0), 1.0 - squared / jnp.float32(radius * radius))
    return falloff * falloff


def advance(padded, latitude, lat_count):
    centre = padded[:, :, 1:-1]
    northern = padded[:, :, 2:]
    southern = padded[:, :, :-2]
    eastern = jnp.roll(centre, -1, axis=3)
    western = jnp.roll(centre, 1, axis=3)
    flux_east = (1.0 + padded[:, 0]) * padded[:, 1]
    flux_north = (1.0 + padded[:, 0]) * padded[:, 2]
    mid_east = flux_east[:, 1:-1]
    divergence = (jnp.roll(mid_east, -1, axis=2) - jnp.roll(mid_east, 1, axis=2)) / 2.0
    divergence = divergence + (flux_north[:, 2:] - flux_north[:, :-2]) / 2.0
    along_lon = (eastern - western) / 2.0
    along_lat = (northern - southern) / 2.0
    eastward = centre[:, 1]
    northward = centre[:, 2]
    coriolis = 0.8 * jnp.sin(jnp.pi * ((latitude.astype(jnp.float32) + 0.5) / lat_count - 0.5))
    coriolis = coriolis[None, :, None]
    tend_east = (
        eastward * along_lon[:, 1]
        + northward * along_lat[:, 1]
        + along_lon[:, 0]
        - coriolis * northward
    )
    tend_north = (
        eastward * along_lon[:, 2]
        + northward * along_lat[:, 2]
        + along_lat[:, 0]
        + coriolis * eastward
    )
    tendency = jnp.stack([divergence, tend_east, tend_north], axis=1)
    return 0.25 * (northern + southern + eastern + western) - time_step * tendency


def local(ensemble, weights, obs_column):
    row_count = ensemble.shape[0]
    members = ensemble.shape[1]
    lat_here = row_count // (3 * NLON)
    lat_count = lat_here * lax.axis_size("st")
    predicted_rows = ensemble.astype(jnp.float32)
    ensemble_mean = jnp.mean(predicted_rows, axis=1, keepdims=True)
    member_anomalies = (predicted_rows - ensemble_mean).astype(jnp.bfloat16)
    row_start = lax.axis_index("st") * row_count
    offset = obs_column - row_start
    inside_band = (offset >= 0) & (offset < row_count)
    clipped = jnp.clip(offset, 0, row_count - 1)
    picked = jnp.take(member_anomalies, clipped, axis=0)
    partial_value = jnp.where(inside_band[:, None], picked, jnp.zeros_like(picked)).astype(
        jnp.float32
    )
    obs_anom = lax.psum(partial_value.astype(jnp.bfloat16), "st")
    state_rows = row_start + jnp.arange(row_count, dtype=jnp.int32)
    covariance = lax.dot_general(
        member_anomalies, obs_anom, (((1,), (1,)), ((), ())), preferred_element_type=jnp.float32
    )
    kalman_gain = (
        covariance * tapering(state_rows, obs_column, lat_count) / jnp.float32(members - 1)
    ).astype(jnp.bfloat16)
    state_update = jnp.dot(kalman_gain, weights, preferred_element_type=jnp.float32)
    first_member = lax.axis_index("ob") * MEMBERS_PER_PART
    local_rows = lax.dynamic_slice_in_dim(predicted_rows, first_member, MEMBERS_PER_PART, 1)
    shared = lax.psum_scatter(state_update, "ob", scatter_dimension=1, tiled=True)
    updated_members = local_rows + shared
    fields = updated_members.reshape(lat_here, 3, NLON, MEMBERS_PER_PART).transpose(3, 1, 0, 2)
    band_start = lax.axis_index("st") * lat_here
    extended = with_halo(fields, (("st", 2),), STEPS)
    first_row = band_start - STEPS
    for section in range(STEPS):
        kept = extended.shape[2] - 2
        latitude = first_row + section + 1 + jnp.arange(kept, dtype=jnp.int32)
        extended = advance(extended, latitude, lat_count)
        inside = (latitude >= 0) & (latitude < lat_count)
        extended = jnp.where(inside[None, None, :, None], extended, jnp.float32(0.0))
    fields = extended
    return fields


def solution(mesh):
    return jax.shard_map(
        local,
        mesh=mesh,
        in_specs=(P("st", None), P("ob", None), P("ob")),
        out_specs=P("ob", None, "st", None),
        check_vma=False,
    )
```

profile of v0, /device:TPU:8, one launch (start us, length us, event | category | flops | bytes accessed | tf_op | source)
XLA Modules:
  0.0 139.1 jit_solution(10574656669796040680)
XLA Ops:
  6.5 0.7 add_select_fusion.3
  7.3 0.7 compare_and_fusion.1
  8.0 1.0 convert_reduce_fusion
  9.0 1.0 subtract_convert_fusion
  10.0 0.3 copy.60
  10.4 3.2 %gather_fusion = bf16[1024,64]{1,0:T(8,128)(2,1)S(1)} fusion(bf16[2304,64]{1,0:T(8,128)(2,1)S(1)} %copy.60, s32[1024]{0:T(1024)S(1)} %get-tuple-element.44), kind=kCustom, calls=%fused_computation | custom fusion | bytes 266240 | tf_op jit(solution)/shard_map/jit(_take)/gather | solution.py:83
  13.6 1.0 select_select_fusion
  14.7 71.7 %all-reduce.2.cloned.1.call-done = bf16[1024,64]{1,0:T(8,128)(2,1)} async-done(((bf16[1024,64]{1,0:T(8,128)(2,1)}), bf16[1024,64]{1,0:T(8,128)(2,1)}) %all-reduce.2.cloned.1.call-update) | async-done | bytes 131088 | tf_op jit(solution)/shard_map/psum | solution.py:87
  86.4 8.5 %fusion.10 = f32[2304,64]{0,1:T(8,128)} fusion(bf16[1024,64]{0,1:T(8,128)(2,1)S(1)} %copy-done, bf16[2304,64]{0,1:T(8,128)(2,1)S(1)} %subtract_convert_fusion, bf16[1024,64]{1,0:T(8,128)(2,1)} %all-reduce.2.cloned.1.call-done, s32[1024]{0:T(1024)S(1)} %get-tuple-element.45, s32[2304]{0:T(1024)S(1)} %get-tuple-element.48, s32[1024]{0:T(1024)S(1)} %get-tuple-element.43, ...), kind=kOutput, calls=%fused_computation.12 | convolution fusion | flops 641728512 | bytes 1173504 | tf_op jit(solution)/shard_map/dot_general | solution.py:95
  95.0 0.9 copy-done.1
  96.1 20.7 %reduce-scatter.2.cloned.1.call-done = f32[2304,16]{0,1:T(8,128)} async-done(((f32[2304,64]{0,1:T(8,128)}), f32[2304,16]{0,1:T(8,128)}) %reduce-scatter.2.cloned.1.call-update) | async-done | bytes 147472 | tf_op jit(solution)/shard_map/reduce_scatter | solution.py:98
  116.9 0.9 dynamic-slice_add_fusion
  117.9 3.3 %collective-permute-start.1 = (f32[16,3,3,128]{3,0,2,1:T(8,128)S(1)}, f32[16,3,3,128]{3,0,2,1:T(8,128)S(1)}, u32[]{:S(2)}, u32[]{:S(2)}) collective-permute-start(f32[16,3,3,128]{3,0,2,1:T(8,128)S(1)} %get-tuple-element.30), channel_id=1, source_target_pairs={{4,0},{8,4},{12,8},{16,12},{20,16},{24,20},{28,24},{5,1},{9,5},{13... | collective-permute-start | bytes 221192 | tf_op jit(solution)/shard_map/ppermute | solution.py:20
  121.3 2.5 %collective-permute-start = (f32[16,3,3,128]{3,0,2,1:T(8,128)S(1)}, f32[16,3,3,128]{3,0,2,1:T(8,128)S(1)}, u32[]{:S(2)}, u32[]{:S(2)}) collective-permute-start(f32[16,3,3,128]{3,0,2,1:T(8,128)S(1)} %get-tuple-element.29), channel_id=1, source_target_pairs={{0,4},{4,8},{8,12},{12,16},{16,20},{20,24},{24,28},{1,5},{5,9},{9,... | collective-permute-start | bytes 221192 | tf_op jit(solution)/shard_map/ppermute | solution.py:17
  123.8 0.4 collective-permute-done.1
  124.2 4.3 %collective-permute-done = f32[16,3,3,128]{3,0,2,1:T(8,128)S(1)} collective-permute-done((f32[16,3,3,128]{3,0,2,1:T(8,128)S(1)}, f32[16,3,3,128]{3,0,2,1:T(8,128)S(1)}, u32[]{:S(2)}, u32[]{:S(2)}) %collective-permute-start) | collective-permute-done | bytes 73760 | tf_op jit(solution)/shard_map/ppermute | solution.py:17
  128.5 0.1 fusion.57
  128.6 0.1 fusion.58
  129.0 0.2 subtract_multiply_fusion.1
  129.4 0.2 fusion.12
  130.1 0.2 subtract_multiply_fusion.3
  130.4 0.2 fusion.14
  131.0 0.2 subtract_multiply_fusion.5
  131.4 0.8 fusion.16
  (42 shorter events, 2.0 us)
Async XLA Ops:
  6.5 79.9 %copy-start = (bf16[1024,64]{0,1:T(8,128)(2,1)S(1)}, bf16[1024,64]{0,1:T(8,128)(2,1)}, u32[]{:S(2)}) copy-start(bf16[1024,64]{0,1:T(8,128)(2,1)} %param.4) | copy-start | bytes 393220
  6.5 79.9 %all-reduce.2.cloned.1.call-start = ((), (), s32[]{:S(2)}) async-start(), calls=%async_computation.1 | async-start | bytes 524288 | tf_op jit(solution)/shard_map/psum | solution.py:87
  14.6 102.2 %reduce-scatter.2.cloned.1.call-start = ((), (), s32[]{:S(2)}) async-start(), calls=%async_computation.2 | async-start | bytes 737280 | tf_op jit(solution)/shard_map/reduce_scatter | solution.py:98
  94.9 1.0 copy-start.1
  117.9 6.2 %collective-permute-start.1 = (f32[16,3,3,128]{3,0,2,1:T(8,128)S(1)}, f32[16,3,3,128]{3,0,2,1:T(8,128)S(1)}, u32[]{:S(2)}, u32[]{:S(2)}) collective-permute-start(f32[16,3,3,128]{3,0,2,1:T(8,128)S(1)} %get-tuple-element.30), channel_id=1, source_target_pairs={{4,0},{8,4},{12,8},{16,12},{20,16},{24,20},{28,24},{5,1},{9,5},{13... | collective-permute-start | bytes 221192 | tf_op jit(solution)/shard_map/ppermute | solution.py:20
  121.3 7.1 %collective-permute-start = (f32[16,3,3,128]{3,0,2,1:T(8,128)S(1)}, f32[16,3,3,128]{3,0,2,1:T(8,128)S(1)}, u32[]{:S(2)}, u32[]{:S(2)}) collective-permute-start(f32[16,3,3,128]{3,0,2,1:T(8,128)S(1)} %get-tuple-element.29), channel_id=1, source_target_pairs={{0,4},{4,8},{8,12},{12,16},{16,20},{20,24},{24,28},{1,5},{5,9},{9,... | collective-permute-start | bytes 221192 | tf_op jit(solution)/shard_map/ppermute | solution.py:17
Sparse Core Ops, SparseCore 0:
  14.8 71.6 all-reduce.1
  95.1 21.7 reduce-scatter.1
where the time goes:
time: 139 us
  waiting for transfers between devices  97.1 us (70%)
  between operations  13.7 us (10%)
  matrix products  8.5 us (6%)
  other arithmetic  8.14 us (6%)
  starting transfers between devices  5.89 us (4%)
  local copies, waits for them, and re-layouts  5.74 us (4%)
    psum x1, waiting for transfers between devices, local(): obs_anom = lax.psum(partial_value.astype(jnp.bfloat16), 'st')  71.7 us
    reduce_scatter x1, waiting for transfers between devices, local(): lax.psum_scatter(state_update, 'ob', scatter_dimension=1, tiled=True)  20.7 us
    dot_general x1, matrix products, local(): jnp.dot(kalman_gain, weights, preferred_element_type=jnp.float32)  8.5 us
    ppermute x1, waiting for transfers between devices, with_halo(): lax.ppermute(lax.slice_in_dim(block, block.shape[dim] - width, None, axis...  4.25 us
    ppermute x1, starting transfers between devices, with_halo(): lax.ppermute(lax.slice_in_dim(block, 0, width, axis=dim), axis, backward)  3.35 us
    gather x1, local copies, waits for them, and re-layouts, local(): picked = jnp.take(member_anomalies, clipped, axis=0)  3.21 us
  transfers between devices with their start and end apart: 4, of which 4 were waited for; matrix products, arithmetic and copies ran while one was open for 0% of the time, Pallas kernels for 0%

commit v1 on v0

--- a/solution.py
+++ b/solution.py
@@ -84,7 +84,7 @@
     partial_value = jnp.where(inside_band[:, None], picked, jnp.zeros_like(picked)).astype(
         jnp.float32
     )
-    obs_anom = lax.psum(partial_value.astype(jnp.bfloat16), "st")
+    obs_anom = jnp.sum(lax.all_gather(partial_value.astype(jnp.bfloat16), "st"), axis=0)
     state_rows = row_start + jnp.arange(row_count, dtype=jnp.int32)
     covariance = lax.dot_general(
         member_anomalies, obs_anom, (((1,), (1,)), ((), ())), preferred_element_type=jnp.float32

time: 139 us -> 108 us (0.78)
  waiting for transfers between devices: 97.1 us -> 66.8 us
    psum x1 -> x0, waiting for transfers between devices: 71.7 us -> none  [local(): obs_anom = lax.psum(partial_value.astype(jnp.bfloat16), 'st')]
    all_gather x0 -> x1, waiting for transfers between devices: none -> 40.4 us  [local(): lax.all_gather(partial_value.astype(jnp.bfloat16), 'st')]
    reduce_sum x0 -> x1, other arithmetic: none -> 1.41 us  [local(): jnp.sum(lax.all_gather(partial_value.astype(jnp.bfloat16), 'st'), axis=0)]
where the time goes in v1:
time: 108 us
  waiting for transfers between devices  66.8 us (62%)
  between operations  13.7 us (13%)
  other arithmetic  8.85 us (8%)
  matrix products  7.27 us (7%)
  starting transfers between devices  5.89 us (5%)
  local copies, waits for them, and re-layouts  5.6 us (5%)
    all_gather x1, waiting for transfers between devices, local(): lax.all_gather(partial_value.astype(jnp.bfloat16), 'st')  40.4 us
    reduce_scatter x1, waiting for transfers between devices, local(): lax.psum_scatter(state_update, 'ob', scatter_dimension=1, tiled=True)  21.8 us
    dot_general x1, matrix products, local(): jnp.dot(kalman_gain, weights, preferred_element_type=jnp.float32)  7.27 us
    ppermute x1, waiting for transfers between devices, with_halo(): lax.ppermute(lax.slice_in_dim(block, block.shape[dim] - width, None, axis...  4.26 us
    ppermute x1, starting transfers between devices, with_halo(): lax.ppermute(lax.slice_in_dim(block, 0, width, axis=dim), axis, backward)  3.35 us
    gather x1, local copies, waits for them, and re-layouts, local(): picked = jnp.take(member_anomalies, clipped, axis=0)  3.21 us
    ppermute x1, starting transfers between devices, with_halo(): lax.ppermute(lax.slice_in_dim(block, block.shape[dim] - width, None, axis...  2.49 us
  transfers between devices with their start and end apart: 4, of which 4 were waited for; matrix products, arithmetic and copies ran while one was open for 0% of the time, Pallas kernels for 0%

profile of v1, /device:TPU:8, one launch (start us, length us, event | category | flops | bytes accessed | tf_op | source)
XLA Modules:
  0.0 108.2 jit_solution(7016573877475819160)
XLA Ops:
  6.5 0.7 add_select_fusion.3
  7.3 0.7 compare_and_fusion.1
  8.0 1.0 convert_reduce_fusion
  9.0 1.0 subtract_convert_fusion
  10.0 0.3 copy.88
  10.4 3.2 %gather_fusion = bf16[1024,64]{1,0:T(8,128)(2,1)S(1)} fusion(bf16[2304,64]{1,0:T(8,128)(2,1)S(1)} %copy.88, s32[1024]{0:T(1024)S(1)} %get-tuple-element.44), kind=kCustom, calls=%fused_computation | custom fusion | bytes 266240 | tf_op jit(solution)/shard_map/jit(_take)/gather | solution.py:83
  13.6 0.3 fusion.11
  13.9 0.8 copy.89
  14.8 40.4 %all-gather.2.cloned.1.call-done = bf16[8,1024,64]{1,2,0:T(8,128)(2,1)} async-done(((bf16[1,1024,64]{1,2,0:T(8,128)(2,1)}), bf16[8,1024,64]{1,2,0:T(8,128)(2,1)}) %all-gather.2.cloned.1.call-update) | async-done | bytes 1048592 | tf_op jit(solution)/shard_map/all_gather | solution.py:87
  55.2 1.4 %reduce_sum.22 = bf16[1024,64]{0,1:T(8,128)(2,1)S(1)} reduce(bf16[8,1024,64]{1,2,0:T(8,128)(2,1)} %all-gather.2.cloned.1.call-done, bf16[]{:T(256)} %constant.85.clone.1), dimensions={0}, to_apply=%region_1.2 | reduce | flops 458752 | bytes 1179650 | tf_op jit(solution)/shard_map/reduce_sum | solution.py:87
  56.6 7.3 %fusion.10 = f32[2304,64]{0,1:T(8,128)} fusion(bf16[1024,64]{0,1:T(8,128)(2,1)S(1)} %copy-done, bf16[2304,64]{0,1:T(8,128)(2,1)S(1)} %subtract_convert_fusion, bf16[1024,64]{0,1:T(8,128)(2,1)S(1)} %reduce_sum.22, s32[1024]{0:T(1024)S(1)} %get-tuple-element.45, s32[2304]{0:T(1024)S(1)} %get-tuple-element.48, s32[1024]{0:T(1024)S(1)} %get-tuple-element.43, ...), kind=kOutput, calls=%fused_computation.12 | convolution fusion | flops 641728512 | bytes 1173504 | tf_op jit(solution)/shard_map/dot_general | solution.py:95
  64.1 21.8 %reduce-scatter.2.cloned.1.call-done = f32[2304,16]{0,1:T(8,128)} async-done(((f32[2304,64]{0,1:T(8,128)}), f32[2304,16]{0,1:T(8,128)}) %reduce-scatter.2.cloned.1.call-update) | async-done | bytes 147472 | tf_op jit(solution)/shard_map/reduce_scatter | solution.py:98
  86.0 0.9 dynamic-slice_add_fusion
  87.0 3.4 %collective-permute-start.1 = (f32[16,3,3,128]{3,0,2,1:T(8,128)S(1)}, f32[16,3,3,128]{3,0,2,1:T(8,128)S(1)}, u32[]{:S(2)}, u32[]{:S(2)}) collective-permute-start(f32[16,3,3,128]{3,0,2,1:T(8,128)S(1)} %get-tuple-element.30), channel_id=1, source_target_pairs={{4,0},{8,4},{12,8},{16,12},{20,16},{24,20},{28,24},{5,1},{9,5},{13... | collective-permute-start | bytes 221192 | tf_op jit(solution)/shard_map/ppermute | solution.py:20
  90.4 2.5 %collective-permute-start = (f32[16,3,3,128]{3,0,2,1:T(8,128)S(1)}, f32[16,3,3,128]{3,0,2,1:T(8,128)S(1)}, u32[]{:S(2)}, u32[]{:S(2)}) collective-permute-start(f32[16,3,3,128]{3,0,2,1:T(8,128)S(1)} %get-tuple-element.29), channel_id=1, source_target_pairs={{0,4},{4,8},{8,12},{12,16},{16,20},{20,24},{24,28},{1,5},{5,9},{9,... | collective-permute-start | bytes 221192 | tf_op jit(solution)/shard_map/ppermute | solution.py:17
  92.9 0.4 collective-permute-done.1
  93.3 4.3 %collective-permute-done = f32[16,3,3,128]{3,0,2,1:T(8,128)S(1)} collective-permute-done((f32[16,3,3,128]{3,0,2,1:T(8,128)S(1)}, f32[16,3,3,128]{3,0,2,1:T(8,128)S(1)}, u32[]{:S(2)}, u32[]{:S(2)}) %collective-permute-start) | collective-permute-done | bytes 73760 | tf_op jit(solution)/shard_map/ppermute | solution.py:17
  97.7 0.1 fusion.59
  98.1 0.2 subtract_multiply_fusion.1
  98.5 0.2 fusion.13
  99.2 0.2 subtract_multiply_fusion.3
  99.5 0.2 fusion.15
  100.2 0.2 subtract_multiply_fusion.5
  100.5 0.8 fusion.17
  (44 shorter events, 2.2 us)
Async XLA Ops:
  6.5 50.0 %copy-start = (bf16[1024,64]{0,1:T(8,128)(2,1)S(1)}, bf16[1024,64]{0,1:T(8,128)(2,1)}, u32[]{:S(2)}) copy-start(bf16[1024,64]{0,1:T(8,128)(2,1)} %param.4) | copy-start | bytes 393220
  6.5 48.6 %all-gather.2.cloned.1.call-start = ((), (), s32[]{:S(2)}) async-start(), calls=%async_computation.1 | async-start | bytes 1179648 | tf_op jit(solution)/shard_map/all_gather | solution.py:87
  14.7 71.2 %reduce-scatter.2.cloned.1.call-start = ((), (), s32[]{:S(2)}) async-start(), calls=%async_computation.2 | async-start | bytes 737280 | tf_op jit(solution)/shard_map/reduce_scatter | solution.py:98
  56.6 7.3 %copy-start.1 = (bf16[2304,64]{0,1:T(8,128)(2,1)S(1)}, bf16[2304,64]{0,1:T(8,128)(2,1)}, u32[]{:S(2)}) copy-start(bf16[2304,64]{0,1:T(8,128)(2,1)} %param.3) | copy-start | bytes 884740
  87.0 6.2 %collective-permute-start.1 = (f32[16,3,3,128]{3,0,2,1:T(8,128)S(1)}, f32[16,3,3,128]{3,0,2,1:T(8,128)S(1)}, u32[]{:S(2)}, u32[]{:S(2)}) collective-permute-start(f32[16,3,3,128]{3,0,2,1:T(8,128)S(1)} %get-tuple-element.30), channel_id=1, source_target_pairs={{4,0},{8,4},{12,8},{16,12},{20,16},{24,20},{28,24},{5,1},{9,5},{13... | collective-permute-start | bytes 221192 | tf_op jit(solution)/shard_map/ppermute | solution.py:20
  90.4 7.1 %collective-permute-start = (f32[16,3,3,128]{3,0,2,1:T(8,128)S(1)}, f32[16,3,3,128]{3,0,2,1:T(8,128)S(1)}, u32[]{:S(2)}, u32[]{:S(2)}) collective-permute-start(f32[16,3,3,128]{3,0,2,1:T(8,128)S(1)} %get-tuple-element.29), channel_id=1, source_target_pairs={{0,4},{4,8},{8,12},{12,16},{16,20},{20,24},{24,28},{1,5},{5,9},{9,... | collective-permute-start | bytes 221192 | tf_op jit(solution)/shard_map/ppermute | solution.py:17
Sparse Core Ops, SparseCore 0:
  14.8 40.2 all-gather.1
  64.0 21.9 reduce-scatter.1
